TPU v7x, 512 devices: a whole 4x4x16 slice. The times are simulated.
512 devices in a mesh: grid: 32 (over y, x, core), pts: 16 (over z).
Axes of the slice: x: 4, y: 4, z: 16, core: 2. Of those that a mesh axis runs over, the one named last changes fastest.
Arguments:
- orbitals: bfloat16 [512, 16384], P(None, 'grid'), may hold values from -0.8984375 to 0.8984375
- point_index: int32 [8192], P('pts'), may hold values from 0 to 16383
Outputs:
- screened: float32 [16, 512, 128, 128], P('pts', 'grid')
All inputs are finite; a program needn't handle non-finite values.
Results may differ from a plain program's by a relative error of at most 0.0003.
Values may be sent and summed in bfloat16 or wider, within the bound.
A program may use at most 64 MiB of HBM per device.

v0:
```python
import math

import jax
import jax.numpy as jnp
from jax import lax
from jax.sharding import PartitionSpec as P

SIDE = 128


HIGHEST_PRECISION = lax.Precision.HIGHEST


def dft_tables():
    product_index = (
        lax.broadcasted_iota(jnp.int32, (SIDE, SIDE), 0)
        * lax.broadcasted_iota(jnp.int32, (SIDE, SIDE), 1)
        % SIDE
    )
    angles = product_index.astype(jnp.float32) * (2.0 * math.pi / SIDE)
    return (jnp.cos(angles), jnp.sin(angles))


def screen_kernel():
    frequency = jnp.arange(SIDE, dtype=jnp.int32)
    wavenumber = jnp.minimum(frequency, SIDE - frequency).astype(jnp.float32)
    screening = SIDE / 16.0
    values = screening / jnp.sqrt(
        wavenumber[:, None] ** 2 + wavenumber[None, :] ** 2 + screening * screening
    )
    anchor = (frequency[:, None] == 0) & (frequency[None, :] == 0)
    return jnp.where(anchor, jnp.zeros_like(values), values)


def column_pass(values, matrix):
    return jnp.einsum("kx,nxy->nky", matrix, values, precision=HIGHEST_PRECISION)


def screen_sheets(stacked, cos_table, sin_table, kernel_values):
    sheets = stacked[0, :, 0]
    real_rows = jnp.dot(sheets, cos_table, precision=HIGHEST_PRECISION)
    imag_rows = -jnp.dot(sheets, sin_table, precision=HIGHEST_PRECISION)
    real_full = column_pass(real_rows, cos_table) + column_pass(imag_rows, sin_table)
    imag_full = column_pass(imag_rows, cos_table) - column_pass(real_rows, sin_table)
    real_scaled = real_full * kernel_values
    imag_scaled = imag_full * kernel_values
    real_back = column_pass(real_scaled, cos_table) - column_pass(imag_scaled, sin_table)
    imag_back = column_pass(imag_scaled, cos_table) + column_pass(real_scaled, sin_table)
    result = jnp.dot(real_back, cos_table, precision=HIGHEST_PRECISION) - jnp.dot(
        imag_back, sin_table, precision=HIGHEST_PRECISION
    )
    return (result * (1.0 / (SIDE * SIDE)))[None]


def shards(orbitals, point_index):
    cell_count = orbitals.shape[1]
    tile_points = point_index.shape[0]
    grid_count = lax.axis_size("grid")
    row_count = cell_count // SIDE
    local_index = point_index - lax.axis_index("grid") * cell_count
    owner_mask = (
        lax.broadcasted_iota(jnp.int32, (cell_count, tile_points), 0) == local_index[None, :]
    ).astype(jnp.bfloat16)
    own_values = jnp.dot(orbitals, owner_mask, preferred_element_type=jnp.float32)
    picked = lax.psum(own_values.astype(jnp.bfloat16), "grid")
    pair_values = lax.dot_general(
        picked, orbitals, (((0,), (0,)), ((), ())), preferred_element_type=jnp.float32
    )
    squared = pair_values * pair_values
    cos_table, sin_table = dft_tables()
    kernel_values = screen_kernel()
    tile_block = squared.reshape(grid_count, tile_points // grid_count, row_count, SIDE)
    stacked = tile_block[:, :, None]
    arrived = lax.all_to_all(stacked, "grid", split_axis=0, concat_axis=3, tiled=True)
    return screen_sheets(arrived, cos_table, sin_table, kernel_values)


def solution(mesh):
    in_specs = (P(None, "grid"), P("pts"))
    out_specs = P("pts", "grid", None, None)
    return jax.shard_map(shards, mesh=mesh, in_specs=in_specs, out_specs=out_specs, check_vma=False)
```

profile of v0, /device:TPU:1, one launch (start us, length us, event | category | flops | bytes accessed | tf_op | source)
XLA Modules:
  0.0 201.5 jit_solution(8437123184860261260)
XLA Ops:
  6.5 0.0 copy-start
  6.5 0.0 all-reduce.2.cloned.1.call-start
  6.5 0.0 copy-start.1
  6.5 0.7 copy-done.1
  7.3 0.3 copy-done
  7.6 1.3 fusion.8
  8.9 0.0 all-reduce.2.cloned.1.call-update
  8.9 141.9 %all-reduce.2.cloned.1.call-done = bf16[512,512]{0,1:T(8,128)(2,1)} async-done(((bf16[512,512]{0,1:T(8,128)(2,1)}), bf16[512,512]{0,1:T(8,128)(2,1)}) %all-reduce.2.cloned.1.call-update) | async-done | bytes 524304 | tf_op jit(solution)/shard_map/psum | solution.py:65
  150.8 1.5 convolution_multiply_fusion
  152.3 1.3 broadcast_in_dim_reshape.3
  153.6 6.0 %all-to-all-start = ((f32[32,16,1,4,128]{4,3,1,2,0:T(4,128)}), f32[32,16,1,4,128]{4,3,1,2,0:T(4,128)S(1)}, u32[]{:S(2)}, u32[]{:S(2)}) async-start(f32[32,16,1,4,128]{4,3,1,2,0:T(4,128)} %bitcast.1), calls=%async_computation | async-start | bytes 2097152 | tf_op jit(solution)/shard_map/all_to_all | solution.py:74
  159.7 0.1 multiply_select_fusion
  159.8 16.9 %all-to-all-done = f32[32,16,1,4,128]{4,3,1,2,0:T(4,128)S(1)} async-done(((f32[32,16,1,4,128]{4,3,1,2,0:T(4,128)}), f32[32,16,1,4,128]{4,3,1,2,0:T(4,128)S(1)}, u32[]{:S(2)}, u32[]{:S(2)}) %all-to-all-start) | async-done | bytes 1048608 | tf_op jit(solution)/shard_map/all_to_all | solution.py:74
  176.7 0.3 copy.9
  177.0 1.2 convolution_negate_fusion
  178.2 1.3 fusion.31
  179.5 1.2 fusion.29
  180.8 1.9 fusion.25
  182.7 1.9 fusion.7
  184.6 1.2 fusion.5
  185.9 1.3 fusion.21
  187.2 1.3 fusion.27
  188.5 1.5 fusion.2
  189.9 1.3 fusion.3
  191.2 1.2 fusion.23
  192.5 2.2 %fusion.1 = f32[1,16,128,128]{3,2,1,0:T(8,128)} fusion(f32[16,128,128]{2,1,0:T(8,128)S(1)} %fusion.23, f32[16,128,128]{2,1,0:T(8,128)S(1)} %fusion.2), kind=kOutput, calls=%fused_computation.3 | convolution fusion | flops 403406848 | bytes 3145728 | tf_op jit(solution)/shard_map/dot_general | solution.py:49
  (3 shorter events, 0.0 us)
Async XLA Ops:
  6.5 1.1 copy-start
  6.5 144.3 %all-reduce.2.cloned.1.call-start = ((), (), s32[]{:S(2)}) async-start(), calls=%async_computation.1 | async-start | bytes 1048576 | tf_op jit(solution)/shard_map/psum | solution.py:65
  6.5 0.7 copy-start.1
  153.6 23.1 %all-to-all-start = ((f32[32,16,1,4,128]{4,3,1,2,0:T(4,128)}), f32[32,16,1,4,128]{4,3,1,2,0:T(4,128)S(1)}, u32[]{:S(2)}, u32[]{:S(2)}) async-start(f32[32,16,1,4,128]{4,3,1,2,0:T(4,128)} %bitcast.1), calls=%async_computation | async-start | bytes 2097152 | tf_op jit(solution)/shard_map/all_to_all | solution.py:74
Sparse Core Ops, SparseCore 0:
  10.5 140.2 all-reduce.1
where the time goes:
time: 202 us; the launch traced here: 201 us
  waiting for transfers between devices  159 us (79%)
  matrix products  20.4 us (10%)
  between operations  13.5 us (7%)
  starting transfers between devices  6.02 us (3%)
  local copies, waits for them, and re-layouts  2.62 us (1%)
    psum x1, waiting for transfers between devices, shards(): picked = lax.psum(own_values.astype(jnp.bfloat16), 'grid')  142 us
    all_to_all x1, waiting for transfers between devices, shards(): lax.all_to_all(stacked, 'grid', split_axis=0, concat_axis=3, tiled=True)  16.9 us
    dot_general x8, matrix products, column_pass(): jnp.einsum('kx,nxy->nky', matrix, values, precision=HIGHEST_PRECISION)  11.6 us
    all_to_all x1, starting transfers between devices, shards(): lax.all_to_all(stacked, 'grid', split_axis=0, concat_axis=3, tiled=True)  6.02 us
  transfers between devices with their start and end apart: 2, of which 2 were waited for; matrix products, arithmetic and copies ran while one was open for 0% of the time, Pallas kernels for 0%

commit v1 on v0

v1 whole, which is shorter than its diff:
```python
import functools
import math

import jax
import jax.numpy as jnp
from jax import lax
from jax.experimental import pallas as pl
from jax.experimental.pallas import tpu as pltpu
from jax.sharding import PartitionSpec as P

SIDE = 128
MESH = pl.DeviceIdType.MESH
F32 = jnp.float32
BF16 = jnp.bfloat16
TOP = 32766.0
FLOOR = 1e-30


def split(values):
    high = values.astype(BF16)
    return high, (values - high.astype(F32)).astype(BF16)


def cas_table():
    rows = lax.broadcasted_iota(jnp.int32, (SIDE, SIDE), 0)
    columns = lax.broadcasted_iota(jnp.int32, (SIDE, SIDE), 1)
    angles = ((rows * columns) % SIDE).astype(F32) * (2.0 * math.pi / SIDE)
    return jnp.cos(angles) + jnp.sin(angles)


def screen_kernel():
    rows = lax.broadcasted_iota(jnp.int32, (SIDE, SIDE), 0)
    columns = lax.broadcasted_iota(jnp.int32, (SIDE, SIDE), 1)
    across = jnp.minimum(rows, SIDE - rows).astype(F32)
    along = jnp.minimum(columns, SIDE - columns).astype(F32)
    screening = SIDE / 16.0
    values = screening / jnp.sqrt(across * across + along * along + screening * screening)
    return jnp.where((rows == 0) & (columns == 0), 0.0, values * (1.0 / (SIDE * SIDE)))


def offsets(size_y, size_x):
    far = lambda d, n: min(d, n - d)
    every = [(dy, dx) for dy in range(size_y) for dx in range(size_x) if (dy, dx) != (0, 0)]
    return sorted(every, key=lambda o: (far(o[0], size_y) + far(o[1], size_x), o))


def body(
    size_y, size_x, points,
    orb_hbm, idx_hbm, out_ref,
    phi, idx, partial, got, vectors, quant, scale, quant_in, scale_in, rows_done, wide, tall, kern,
    load_sem, sib_send, sib_recv, rs_send, rs_recv, ag_send, ag_recv, q_send, q_recv, s_send, s_recv,
):
    me = lax.axis_index("grid")
    core = me % 2
    chip = me // 2
    my_y = chip // size_x
    my_x = chip % size_x
    chips = size_y * size_x
    cells = phi.shape[2]
    offs = offsets(size_y, size_x)

    def at(dy, dx):
        return ((my_y + dy + size_y) % size_y) * size_x + (my_x + dx + size_x) % size_x

    def device(c):
        return {"grid": c * 2 + core}

    sibling = {"grid": chip * 2 + 1 - core}

    barrier = pltpu.get_barrier_semaphore()
    pl.semaphore_signal(barrier, inc=1, device_id=sibling, device_id_type=MESH)
    for dy, dx in offs:
        pl.semaphore_signal(barrier, inc=1, device_id=device(at(dy, dx)), device_id_type=MESH)

    load_orb = pltpu.make_async_copy(orb_hbm, phi.at[core], load_sem.at[0])
    load_orb.start()
    load_idx = pltpu.make_async_copy(idx_hbm, idx, load_sem.at[1])
    load_idx.start()

    high, low = split(cas_table())
    wide[0:SIDE, 0:SIDE] = high
    wide[0:SIDE, SIDE:] = low
    wide[SIDE:, 0:SIDE] = high
    wide[SIDE:, SIDE:] = low
    tall[0:SIDE, 0:SIDE] = high
    tall[0:SIDE, SIDE:] = high
    tall[SIDE:, 0:SIDE] = low
    tall[SIDE:, SIDE:] = low
    kern[...] = screen_kernel()

    load_idx.wait()
    total = idx.shape[1]
    column = jnp.transpose(jnp.broadcast_to(idx[...], (SIDE, total)))
    column = column.reshape(chips, 2, points, SIDE)
    column = jnp.where(core == 0, column[:, 0], column[:, 1]).reshape(chips * points, SIDE)
    column = column - chip * (2 * cells)
    lane = lax.broadcasted_iota(jnp.int32, (chips * points, SIDE), 1)

    def owned(half):
        parts = [
            jnp.where(column == lane + (half * cells + j * SIDE), 1.0, 0.0).astype(BF16)
            for j in range(cells // SIDE)
        ]
        mask = jnp.concatenate(parts, axis=1)
        return lax.dot_general(mask, phi[half], (((1,), (1,)), ((), ())), preferred_element_type=F32)

    load_orb.wait()
    pl.semaphore_wait(barrier, len(offs) + 1)

    to_sibling = pltpu.make_async_remote_copy(
        src_ref=phi.at[core], dst_ref=phi.at[core], send_sem=sib_send, recv_sem=sib_recv,
        device_id=sibling, device_id_type=MESH,
    )
    to_sibling.start()
    to_sibling.wait()

    own = (owned(0) + owned(1)).astype(BF16)
    partial[...] = own.reshape(chips, points, own.shape[1])

    def rs_copy(d):
        dy, dx = offs[d]
        peer = at(dy, dx)
        return pltpu.make_async_remote_copy(
            src_ref=partial.at[peer], dst_ref=got.at[d], send_sem=rs_send.at[d], recv_sem=rs_recv.at[d],
            device_id=device(peer), device_id_type=MESH,
        )

    rs = [rs_copy(d) for d in range(len(offs))]
    for copy in reversed(rs):
        copy.start()
    mine = partial[chip].astype(F32)
    for d, copy in enumerate(rs):
        copy.wait_recv()
        mine = mine + got[d].astype(F32)
    vectors[0] = mine.astype(BF16)

    def ag_copy(d):
        dy, dx = offs[d]
        return pltpu.make_async_remote_copy(
            src_ref=vectors.at[0], dst_ref=vectors.at[d + 1], send_sem=ag_send.at[d], recv_sem=ag_recv.at[d],
            device_id=device(at(dy, dx)), device_id_type=MESH,
        )

    ag = [ag_copy(d) for d in range(len(offs))]
    for copy in reversed(ag):
        copy.start()

    def back_copies(d):
        dy, dx = offs[d]
        to = device(at(-dy, -dx))
        first = pltpu.make_async_remote_copy(
            src_ref=quant.at[d + 1], dst_ref=quant_in.at[d + 1], send_sem=q_send.at[d], recv_sem=q_recv.at[d],
            device_id=to, device_id_type=MESH,
        )
        second = pltpu.make_async_remote_copy(
            src_ref=scale.at[d + 1], dst_ref=scale_in.at[d + 1], send_sem=s_send.at[d], recv_sem=s_recv.at[d],
            device_id=to, device_id_type=MESH,
        )
        return first, second

    back = [back_copies(d) for d in range(len(offs))]
    diagonal = lax.broadcasted_iota(jnp.int32, (points, SIDE), 0) == lax.broadcasted_iota(
        jnp.int32, (points, SIDE), 1
    )

    group = 4
    for start in range(0, chips, group):
        for slot in range(start, start + group):
            if slot > 0:
                ag[slot - 1].wait_recv()
        block = vectors[start : start + group].reshape(group * points, vectors.shape[2])
        pair = jnp.concatenate(
            [jnp.dot(block, phi[h], preferred_element_type=F32) for h in range(2)], axis=1
        )
        peak = jnp.maximum(jnp.max(jnp.abs(pair), axis=1, keepdims=True), FLOOR)
        coded = jnp.round(pair * (TOP / peak)).astype(jnp.int32).astype(jnp.int16)
        quant[start : start + group] = coded.reshape(group, points, 2 * cells)
        step = jnp.broadcast_to(peak * (1.0 / TOP), (group * points, SIDE))
        for slot in range(start, start + group):
            piece = step[(slot - start) * points : (slot - start + 1) * points]
            scale[slot] = jnp.sum(jnp.where(diagonal, piece, 0.0), axis=0, keepdims=True)
        for slot in range(start, start + group):
            if slot > 0:
                for copy in back[slot - 1]:
                    copy.start()

    rows = 2 * cells // SIDE

    def along(block, row_of, source):
        step = jnp.sum(
            jnp.where(diagonal, jnp.broadcast_to(row_of, (points, SIDE)), 0.0), axis=1, keepdims=True
        )
        pair = block.astype(jnp.int32).astype(F32) * step
        square = pair * pair
        stacked = jnp.concatenate([square[:, r * SIDE : (r + 1) * SIDE] for r in range(rows)], axis=0)
        high, low = split(stacked)
        product = jnp.dot(jnp.concatenate([high, low], axis=1), wide[...], preferred_element_type=F32)
        at_row = pl.multiple_of(source * (rows * points), rows * points)
        rows_done[pl.ds(at_row, rows * points), :] = product[:, :SIDE] + product[:, SIDE:]

    along(quant[0], scale[0], chip)
    for d in range(len(offs)):
        for copy in back[d]:
            copy.wait_recv()
        dy, dx = offs[d]
        along(quant_in[d + 1], scale_in[d + 1], at(dy, dx))

    weight = jnp.concatenate([kern[...], kern[...]], axis=1)
    for first in range(0, points, 2):
        pieces = [rows_done[pl.ds(p, SIDE, stride=points), :] for p in (first, first + 1)]
        values = jnp.concatenate(pieces, axis=1)
        for turn in range(2):
            high, low = split(values)
            product = jnp.dot(tall[...], jnp.concatenate([high, low], axis=0), preferred_element_type=F32)
            values = product[:SIDE] + product[SIDE:]
            if turn == 0:
                values = values * weight
        high, low = split(values)
        for p in range(2):
            lanes = slice(p * SIDE, (p + 1) * SIDE)
            operand = jnp.concatenate([high[:, lanes], low[:, lanes]], axis=1)
            product = jnp.dot(operand, wide[...], preferred_element_type=F32)
            out_ref[first + p] = product[:, :SIDE] + product[:, SIDE:]

    for copy in rs:
        copy.wait_send()
    for copy in ag:
        copy.wait_send()
    for pair_of in back:
        for copy in pair_of:
            copy.wait_send()


def shards(size_y, size_x, orbitals, point_index):
    orbital_count, cells = orbitals.shape
    chips = size_y * size_x
    points = point_index.shape[0] // (2 * chips)
    others = chips - 1
    dma = pltpu.SemaphoreType.DMA
    out = pl.pallas_call(
        functools.partial(body, size_y, size_x, points),
        out_shape=jax.ShapeDtypeStruct((points, SIDE, SIDE), F32),
        in_specs=[pl.BlockSpec(memory_space=pl.ANY)] * 2,
        out_specs=pl.BlockSpec(memory_space=pltpu.VMEM),
        scratch_shapes=[
            pltpu.VMEM((2, orbital_count, cells), BF16),
            pltpu.VMEM((1, point_index.shape[0]), jnp.int32),
            pltpu.VMEM((chips, points, orbital_count), BF16),
            pltpu.VMEM((others, points, orbital_count), BF16),
            pltpu.VMEM((chips, points, orbital_count), BF16),
            pltpu.VMEM((chips, points, 2 * cells), jnp.int16),
            pltpu.VMEM((chips, 1, SIDE), F32),
            pltpu.VMEM((chips, points, 2 * cells), jnp.int16),
            pltpu.VMEM((chips, 1, SIDE), F32),
            pltpu.VMEM((SIDE * points, SIDE), F32),
            pltpu.VMEM((2 * SIDE, 2 * SIDE), BF16),
            pltpu.VMEM((2 * SIDE, 2 * SIDE), BF16),
            pltpu.VMEM((SIDE, SIDE), F32),
            dma((2,)), dma, dma,
            dma((others,)), dma((others,)), dma((others,)), dma((others,)),
            dma((others,)), dma((others,)), dma((others,)), dma((others,)),
        ],
        compiler_params=pltpu.CompilerParams(collective_id=0, has_side_effects=True),
    )(orbitals, point_index.reshape(1, -1))
    return out[None]


def solution(mesh):
    grid_count = mesh.shape["grid"]
    size = math.isqrt(grid_count // 2)
    in_specs = (P(None, "grid"), P("pts"))
    out_specs = P("pts", "grid", None, None)
    step = functools.partial(shards, size, size)
    return jax.shard_map(step, mesh=mesh, in_specs=in_specs, out_specs=out_specs, check_vma=False)
```

time: 202 us -> 39.6 us (0.20)
  the two profiles are of different devices: /device:TPU:1 before, /device:TPU:24 now
where the time goes in v1:
time: 39.6 us; the launch traced here: 39.5 us
  Pallas kernels  37.2 us (94%)
  local copies, waits for them, and re-layouts  2.3 us (6%)
    pallas_call x1, Pallas kernels, shards(): pl.pallas_call(functools.partial(body, size_y, size_x, points), out_shape...  37.2 us
    unnamed x1, local copies, waits for them, and re-layouts  2.3 us

profile of v1, /device:TPU:24, one launch (start us, length us, event | category | flops | bytes accessed | tf_op | source)
XLA Modules:
  0.0 39.5 jit_solution(15397722811709193426)
XLA Ops:
  0.0 37.2 %shard_map.28 = f32[16,128,128]{2,1,0:T(8,128)} custom-call(bf16[512,512]{1,0:T(8,128)(2,1)} %orb_hbm.1, s32[1,512]{1,0:T(1,128)} %bitcast.3), custom_call_target="tpu_custom_call" | custom-call | tf_op jit(solution)/shard_map/pallas_call | solution.py:240
  37.2 2.3 %copy.4 = f32[1,16,128,128]{3,2,1,0:T(8,128)} copy(f32[1,16,128,128]{3,2,1,0:T(8,128)} %bitcast.2) | data formatting | bytes 2097152

commit v2 on v0

v2 whole, which is shorter than its diff:
```python
import functools
import math

import jax
import jax.numpy as jnp
from jax import lax
from jax.experimental import pallas as pl
from jax.experimental.pallas import tpu as pltpu
from jax.sharding import PartitionSpec as P

SIDE = 128
MESH = pl.DeviceIdType.MESH
F32 = jnp.float32
BF16 = jnp.bfloat16
TOP = 32766.0
FLOOR = 1e-30
PARTS = 2
PAIR_GROUP = 8
ROW_GROUP = 4
VMEM_BYTES = 16 * 1024 * 1024


def split(values):
    high = values.astype(BF16)
    return high, (values - high.astype(F32)).astype(BF16)


def cas_table():
    rows = lax.broadcasted_iota(jnp.int32, (SIDE, SIDE), 0)
    columns = lax.broadcasted_iota(jnp.int32, (SIDE, SIDE), 1)
    angles = ((rows * columns) % SIDE).astype(F32) * (2.0 * math.pi / SIDE)
    return jnp.cos(angles) + jnp.sin(angles)


def screen_kernel():
    rows = lax.broadcasted_iota(jnp.int32, (SIDE, SIDE), 0)
    columns = lax.broadcasted_iota(jnp.int32, (SIDE, SIDE), 1)
    across = jnp.minimum(rows, SIDE - rows).astype(F32)
    along = jnp.minimum(columns, SIDE - columns).astype(F32)
    screening = SIDE / 16.0
    values = screening / jnp.sqrt(across * across + along * along + screening * screening)
    return jnp.where((rows == 0) & (columns == 0), 0.0, values * (1.0 / (SIDE * SIDE)))


def offsets(size_y, size_x):
    far = lambda d, n: min(d, n - d)
    every = [(dy, dx) for dy in range(size_y) for dx in range(size_x) if (dy, dx) != (0, 0)]
    return sorted(every, key=lambda o: (-far(o[0], size_y) - far(o[1], size_x), o))


def body(
    size_y, size_x, points,
    orb_hbm, idx_hbm, out_ref,
    phi, idx, first_sum, partial, got, vectors, quant, scale, quant_in, scale_in, rows_done, wide, tall, kern, middle,
    last,
    load_sem, sib_send, sib_recv, rs_send, rs_recv, ag_send, ag_recv, q_send, q_recv, s_send, s_recv,
):
    me = lax.axis_index("grid")
    core = me % 2
    chip = me // 2
    my_y = chip // size_x
    my_x = chip % size_x
    chips = size_y * size_x
    cells = phi.shape[2]
    offs = offsets(size_y, size_x)
    count = len(offs)
    others = range(count)
    depth = phi.shape[1] // PARTS
    parts = range(PARTS)

    def at(dy, dx):
        return ((my_y + dy + size_y) % size_y) * size_x + (my_x + dx + size_x) % size_x

    def device(c):
        return {"grid": c * 2 + core}

    def remote(src, dst, send, recv, to):
        return pltpu.make_async_remote_copy(
            src_ref=src, dst_ref=dst, send_sem=send, recv_sem=recv, device_id=to, device_id_type=MESH
        )

    def wait_all(ref, sem):
        pltpu.make_async_copy(ref, ref, sem).wait()

    sibling = {"grid": chip * 2 + 1 - core}

    with jax.named_scope("signals"):
        load_orb = pltpu.make_async_copy(orb_hbm, phi.at[core], load_sem.at[0])
        load_orb.start()
        load_idx = pltpu.make_async_copy(idx_hbm, idx, load_sem.at[1])
        load_idx.start()
        barrier = pltpu.get_barrier_semaphore()
        pl.semaphore_signal(barrier, inc=1, device_id=sibling, device_id_type=MESH)
        for dy, dx in offs:
            pl.semaphore_signal(barrier, inc=1, device_id=device(at(dy, dx)), device_id_type=MESH)

    with jax.named_scope("barrier"):
        pl.semaphore_wait(barrier, count + 1)

    def band(p):
        return pl.ds(p * depth, depth)

    to_sibling = [
        remote(orb_hbm.at[band(p)], phi.at[core, band(p)], sib_send.at[p], sib_recv.at[p], sibling) for p in parts
    ]
    for copy in to_sibling:
        copy.start()

    with jax.named_scope("indices"):
        load_idx.wait()
        total = idx.shape[1]
        column = jnp.transpose(jnp.broadcast_to(idx[...], (SIDE, total)))
        column = column.reshape(chips, 2, points, SIDE)
        column = jnp.where(core == 0, column[:, 0], column[:, 1]).reshape(chips * points, SIDE)
        column = column - chip * (2 * cells)
        lane = lax.broadcasted_iota(jnp.int32, (chips * points, SIDE), 1)

    def mask_of(half):
        return jnp.concatenate(
            [
                jnp.where(column == lane + (half * cells + j * SIDE), 1.0, 0.0).astype(BF16)
                for j in range(cells // SIDE)
            ],
            axis=1,
        )

    def owned(mask, values):
        return lax.dot_general(mask, values, (((1,), (1,)), ((), ())), preferred_element_type=F32)

    with jax.named_scope("ownpicks"):
        load_orb.wait()
        first_sum[...] = owned(mask_of(core), phi[core])
        theirs = mask_of(1 - core)

    def rs_copy(p, d):
        peer = at(*offs[d])
        return remote(partial.at[p, peer], got.at[p, d], rs_send, rs_recv.at[p], device(peer))

    for p in parts:
        with jax.named_scope("sibling%d" % p):
            to_sibling[p].wait()
        with jax.named_scope("picks%d" % p):
            lanes = slice(p * depth, (p + 1) * depth)
            own = first_sum[:, lanes] + owned(theirs, phi[1 - core, lanes])
            partial[p] = own.astype(BF16).reshape(chips, points, depth)
            for d in others:
                rs_copy(p, d).start()

    with jax.named_scope("tables"):
        high, low = split(cas_table())
        wide[0:SIDE, 0:SIDE] = high
        wide[0:SIDE, SIDE:] = low
        wide[SIDE:, 0:SIDE] = high
        wide[SIDE:, SIDE:] = low
        tall[0:SIDE, 0:SIDE] = high
        tall[0:SIDE, SIDE:] = high
        tall[SIDE:, 0:SIDE] = low
        tall[SIDE:, SIDE:] = low
        kern[...] = screen_kernel()

    starts = range(0, chips, PAIR_GROUP)

    def ag_copy(p, d):
        return remote(
            vectors.at[p, count], vectors.at[p, d], ag_send, ag_recv.at[p, d // PAIR_GROUP], device(at(*offs[d]))
        )

    for p in parts:
        with jax.named_scope("scatter%d" % p):
            wait_all(got.at[p], rs_recv.at[p])
            mine = partial[p, chip].astype(F32)
            for d in others:
                mine = mine + got[p, d].astype(F32)
            vectors[p, count] = mine.astype(BF16)
            for d in others:
                ag_copy(p, d).start()

    def back_copies(d):
        dy, dx = offs[d]
        to = device(at(-dy, -dx))
        g = d // ROW_GROUP
        first = remote(quant.at[d], quant_in.at[d], q_send, q_recv.at[g], to)
        second = remote(scale.at[d], scale_in.at[d], s_send, s_recv.at[g], to)
        return first, second

    diagonal = lax.broadcasted_iota(jnp.int32, (points, SIDE), 0) == lax.broadcasted_iota(
        jnp.int32, (points, SIDE), 1
    )

    for g, start in enumerate(starts):
        size = min(PAIR_GROUP, chips - start)
        group = range(start, start + size)
        with jax.named_scope("gather%d" % start):
            for p in parts:
                here = pl.ds(start, min(size, count - start))
                wait_all(vectors.at[p, here], ag_recv.at[p, g])
        with jax.named_scope("pairs%d" % start):
            halves = []
            for h in range(2):
                pair = None
                for p in parts:
                    block = vectors[p, start : start + size].reshape(size * points, depth)
                    term = jnp.dot(block, phi[h, band(p)], preferred_element_type=F32)
                    pair = term if pair is None else pair + term
                halves.append(pair)
            pair = jnp.concatenate(halves, axis=1)
            peak = jnp.maximum(jnp.max(jnp.abs(pair), axis=1, keepdims=True), FLOOR)
            coded = jnp.round(pair * (TOP / peak)).astype(jnp.int32).astype(jnp.int16)
            quant[start : start + size] = coded.reshape(size, points, 2 * cells)
            step = jnp.broadcast_to(peak * (1.0 / TOP), (size * points, SIDE))
            for slot in group:
                piece = step[(slot - start) * points : (slot - start + 1) * points]
                scale[slot] = jnp.sum(jnp.where(diagonal, piece, 0.0), axis=0, keepdims=True)
            for slot in group:
                if slot < count:
                    for copy in back_copies(slot):
                        copy.start()

    rows = 2 * cells // SIDE

    def along(blocks):
        stacks = []
        for block, row_of, _ in blocks:
            step = jnp.sum(
                jnp.where(diagonal, jnp.broadcast_to(row_of, (points, SIDE)), 0.0), axis=1, keepdims=True
            )
            pair = block.astype(jnp.int32).astype(F32) * step
            square = pair * pair
            stacks.extend(square[:, r * SIDE : (r + 1) * SIDE] for r in range(rows))
        high, low = split(jnp.concatenate(stacks, axis=0))
        product = jnp.dot(jnp.concatenate([high, low], axis=1), wide[...], preferred_element_type=F32)
        product = product[:, :SIDE] + product[:, SIDE:]
        size = rows * points
        for n, (_, _, source) in enumerate(blocks):
            rows_done[pl.ds(pl.multiple_of(source * size, size), size), :] = product[n * size : (n + 1) * size]

    for g, start in enumerate(range(0, chips, ROW_GROUP)):
        size = min(ROW_GROUP, chips - start)
        with jax.named_scope("wait%d" % start):
            here = pl.ds(start, min(size, count - start))
            wait_all(quant_in.at[here], q_recv.at[g])
            wait_all(scale_in.at[here], s_recv.at[g])
        with jax.named_scope("along%d" % start):
            along([
                (quant_in[s], scale_in[s], at(*offs[s])) if s < count else (quant[s], scale[s], chip)
                for s in range(start, start + size)
            ])

    with jax.named_scope("across"):
        weight = jnp.concatenate([kern[...], kern[...]], axis=1)
        for first in range(0, points, 2):
            pieces = [rows_done[pl.ds(p, SIDE, stride=points), :] for p in (first, first + 1)]
            high, low = split(jnp.concatenate(pieces, axis=1))
            product = jnp.dot(tall[...], jnp.concatenate([high, low], axis=0), preferred_element_type=F32)
            high, low = split((product[:SIDE] + product[SIDE:]) * weight)
            middle[first // 2, 0:SIDE] = high
            middle[first // 2, SIDE:] = low
    with jax.named_scope("inverse"):
        for first in range(0, points, 2):
            product = jnp.dot(tall[...], middle[first // 2], preferred_element_type=F32)
            high, low = split(product[:SIDE] + product[SIDE:])
            for p in range(2):
                lanes = slice(p * SIDE, (p + 1) * SIDE)
                last[first + p, :, 0:SIDE] = high[:, lanes]
                last[first + p, :, SIDE:] = low[:, lanes]
    with jax.named_scope("output"):
        for first in range(0, points, 2):
            product = jnp.dot(
                last[first : first + 2].reshape(2 * SIDE, 2 * SIDE), wide[...], preferred_element_type=F32
            )
            out_ref[first : first + 2] = (product[:, :SIDE] + product[:, SIDE:]).reshape(2, SIDE, SIDE)

    with jax.named_scope("sends"):
        wait_all(got, rs_send)
        wait_all(vectors.at[:, pl.ds(0, count)], ag_send)
        wait_all(quant_in, q_send)
        wait_all(scale_in, s_send)


def shards(size_y, size_x, orbitals, point_index):
    orbital_count, cells = orbitals.shape
    chips = size_y * size_x
    points = point_index.shape[0] // (2 * chips)
    others = chips - 1
    depth = orbital_count // PARTS
    dma = pltpu.SemaphoreType.DMA
    in_place = functools.partial(pltpu.with_memory_space_constraint, memory_space=pltpu.HBM)
    out = pl.pallas_call(
        functools.partial(body, size_y, size_x, points),
        out_shape=jax.ShapeDtypeStruct((points, SIDE, SIDE), F32),
        in_specs=[pl.BlockSpec(memory_space=pltpu.HBM)] * 2,
        out_specs=pl.BlockSpec(memory_space=pltpu.VMEM),
        scratch_shapes=[
            pltpu.VMEM((2, orbital_count, cells), BF16),
            pltpu.VMEM((1, point_index.shape[0]), jnp.int32),
            pltpu.VMEM((chips * points, orbital_count), F32),
            pltpu.VMEM((PARTS, chips, points, depth), BF16),
            pltpu.VMEM((PARTS, others, points, depth), BF16),
            pltpu.VMEM((PARTS, chips, points, depth), BF16),
            pltpu.VMEM((chips, points, 2 * cells), jnp.int16),
            pltpu.VMEM((chips, 1, SIDE), F32),
            pltpu.VMEM((others, points, 2 * cells), jnp.int16),
            pltpu.VMEM((others, 1, SIDE), F32),
            pltpu.VMEM((SIDE * points, SIDE), F32),
            pltpu.VMEM((2 * SIDE, 2 * SIDE), BF16),
            pltpu.VMEM((2 * SIDE, 2 * SIDE), BF16),
            pltpu.VMEM((SIDE, SIDE), F32),
            pltpu.VMEM((points // 2, 2 * SIDE, 2 * SIDE), BF16),
            pltpu.VMEM((points, SIDE, 2 * SIDE), BF16),
            dma((2,)), dma((PARTS,)), dma((PARTS,)),
            dma, dma((PARTS,)), dma, dma((PARTS, pl.cdiv(chips, PAIR_GROUP))),
            dma, dma((pl.cdiv(chips, ROW_GROUP),)), dma, dma((pl.cdiv(chips, ROW_GROUP),)),
        ],
        compiler_params=pltpu.CompilerParams(
            collective_id=0, has_side_effects=True, vmem_limit_bytes=VMEM_BYTES
        ),
    )(in_place(orbitals), in_place(point_index.reshape(1, -1)))
    return out[None]


def solution(mesh):
    grid_count = mesh.shape["grid"]
    size = math.isqrt(grid_count // 2)
    in_specs = (P(None, "grid"), P("pts"))
    out_specs = P("pts", "grid", None, None)
    step = functools.partial(shards, size, size)
    return jax.shard_map(step, mesh=mesh, in_specs=in_specs, out_specs=out_specs, check_vma=False)
```

time: 202 us -> 33 us (0.16)
  waiting for transfers between devices: 159 us -> 0 us
  Pallas kernels: 0 us -> 31.9 us
  matrix products: 20.4 us -> 0 us
  between operations: 13.5 us -> 0.01 us
  starting transfers between devices: 6.02 us -> 0 us
    psum x1 -> x0, waiting for transfers between devices: 142 us -> none  [shards(): picked = lax.psum(own_values.astype(jnp.bfloat16), 'grid')]
    pallas_call x0 -> x1, Pallas kernels: none -> 31.9 us  [shards(): pl.pallas_call(functools.partial(body, size_y, size_x, points), out_shape...]
    dot_general x14 -> x0, matrix products: 20.4 us -> none  [the longest x8 11.6 us: column_pass(): jnp.einsum('kx,nxy->nky', matrix, values, precision=HIGHEST_PRECISION)]
    all_to_all x1 -> x0, waiting for transfers between devices: 16.9 us -> none  [shards(): lax.all_to_all(stacked, 'grid', split_axis=0, concat_axis=3, tiled=True)]
    all_to_all x1 -> x0, starting transfers between devices: 6.02 us -> none  [shards(): lax.all_to_all(stacked, 'grid', split_axis=0, concat_axis=3, tiled=True)]
  transfers between devices with their start and end apart: 2 -> 0, of which waited for: 2 -> 0; matrix products, arithmetic and copies ran while one was open for 0% -> 0% of each run, Pallas kernels for 0% -> 0%
where the time goes in v2:
time: 33 us; the launch traced here: 32.9 us
  Pallas kernels  31.9 us (97%)
  local copies, waits for them, and re-layouts  0.97 us (3%)
    pallas_call x1, Pallas kernels, shards(): pl.pallas_call(functools.partial(body, size_y, size_x, points), out_shape...  31.9 us
    unnamed x1, local copies, waits for them, and re-layouts  0.97 us

profile of v2, /device:TPU:1, one launch (start us, length us, event | category | flops | bytes accessed | tf_op | source)
XLA Modules:
  0.0 32.9 jit_solution(2929990921028328948)
XLA Ops:
  0.0 31.9 %shard_map.28 = f32[16,128,128]{2,1,0:T(8,128)S(1)} custom-call(bf16[512,512]{1,0:T(8,128)(2,1)} %orb_hbm.1, s32[1,512]{1,0:T(1,128)} %bitcast.3), custom_call_target="tpu_custom_call" | custom-call | tf_op jit(solution)/shard_map/pallas_call | solution.py:288
  31.9 1.0 %copy.4 = f32[1,16,128,128]{3,2,1,0:T(8,128)} copy(f32[1,16,128,128]{3,2,1,0:T(8,128)S(1)} %bitcast.2) | data formatting | bytes 2097152

commit v3 on v2

v3 whole, which is shorter than its diff:
```python
import functools
import math

import jax
import jax.numpy as jnp
from jax import lax
from jax.experimental import pallas as pl
from jax.experimental.pallas import tpu as pltpu
from jax.sharding import PartitionSpec as P

SIDE = 128
MESH = pl.DeviceIdType.MESH
F32 = jnp.float32
BF16 = jnp.bfloat16
TOP = 32766.0
FLOOR = 1e-30
COLUMN_GROUPS = ((2, 1), (3, 0))
ROW_GROUP = 4
VMEM_BYTES = 16 * 1024 * 1024


def split(values):
    high = values.astype(BF16)
    return high, (values - high.astype(F32)).astype(BF16)


def cas_table():
    rows = lax.broadcasted_iota(jnp.int32, (SIDE, SIDE), 0)
    columns = lax.broadcasted_iota(jnp.int32, (SIDE, SIDE), 1)
    angles = ((rows * columns) % SIDE).astype(F32) * (2.0 * math.pi / SIDE)
    return jnp.cos(angles) + jnp.sin(angles)


def screen_kernel():
    rows = lax.broadcasted_iota(jnp.int32, (SIDE, SIDE), 0)
    columns = lax.broadcasted_iota(jnp.int32, (SIDE, SIDE), 1)
    across = jnp.minimum(rows, SIDE - rows).astype(F32)
    along = jnp.minimum(columns, SIDE - columns).astype(F32)
    screening = SIDE / 16.0
    values = screening / jnp.sqrt(across * across + along * along + screening * screening)
    return jnp.where((rows == 0) & (columns == 0), 0.0, values * (1.0 / (SIDE * SIDE)))


def offsets(size_y, size_x):
    far = lambda d, n: min(d, n - d)
    every = [(dy, dx) for dy in range(size_y) for dx in range(size_x) if (dy, dx) != (0, 0)]
    return sorted(every, key=lambda o: (-far(o[0], size_y) - far(o[1], size_x), o))


def body(
    side, points,
    orb_hbm, idx_hbm, out_ref,
    phi, idx, mine, theirs, from_sib, part, first_in, summed, second_in, vectors, quant, scale, quant_in, scale_in,
    rows_done, wide, tall, kern, middle, last,
    load_sem, sib_send, sib_recv, orb_send, orb_recv, p_send, first_recv, second_recv, third_recv,
    q_send, q_recv, s_send, s_recv,
):
    me = lax.axis_index("grid")
    core = me % 2
    chip = me // 2
    my_y = chip // side
    my_x = chip % side
    chips = side * side
    cells = phi.shape[2]
    orbital_count = phi.shape[1]
    half = orbital_count // 2
    offs = offsets(side, side)
    count = len(offs)
    steps = [2, 1, 3][-(side - 1) :]
    flavours = range(2)
    first_at = (my_x, my_y)

    def at(dy, dx):
        return ((my_y + dy + side) % side) * side + (my_x + dx + side) % side

    def device(c):
        return {"grid": c * 2 + core}

    def along_first(f, e):
        return device(at(0, e) if f == 0 else at(e, 0))

    def along_second(f, e):
        return device(at(e, 0) if f == 0 else at(0, e))

    def remote(src, dst, send, recv, to):
        return pltpu.make_async_remote_copy(
            src_ref=src, dst_ref=dst, send_sem=send, recv_sem=recv, device_id=to, device_id_type=MESH
        )

    def wait_all(ref, sem):
        pltpu.make_async_copy(ref, ref, sem).wait()

    sibling = {"grid": chip * 2 + 1 - core}

    with jax.named_scope("signals"):
        load_idx = pltpu.make_async_copy(idx_hbm, idx, load_sem.at[1])
        load_idx.start()
        load_orb = pltpu.make_async_copy(orb_hbm, phi.at[core], load_sem.at[0])
        load_orb.start()
        barrier = pltpu.get_barrier_semaphore()
        pl.semaphore_signal(barrier, inc=1, device_id=sibling, device_id_type=MESH)
        for e in steps:
            for f in flavours:
                pl.semaphore_signal(barrier, inc=1, device_id=along_first(f, e), device_id_type=MESH)

    with jax.named_scope("indices"):
        load_idx.wait()
        total = idx.shape[1]
        column = jnp.transpose(jnp.broadcast_to(idx[...], (SIDE, total))) - me * cells
        column = column.reshape(chips, 2, points, SIDE)
        lane = lax.broadcasted_iota(jnp.int32, (chips * points, SIDE), 1)

    def owned(layer, to):
        chosen = jnp.where(layer == 0, column[:, 0], column[:, 1]).reshape(chips * points, SIDE)
        mask = jnp.concatenate(
            [jnp.where(chosen == lane + j * SIDE, 1.0, 0.0).astype(BF16) for j in range(cells // SIDE)], axis=1
        )
        found = lax.dot_general(mask, phi[core], (((1,), (1,)), ((), ())), preferred_element_type=F32)
        found = found.astype(BF16)
        for y in range(side):
            for x in range(side):
                rows = slice((y * side + x) * points, (y * side + x + 1) * points)
                to[0, x, y] = found[rows, :half]
                to[1, y, x] = found[rows, half:]

    with jax.named_scope("ownpicks"):
        load_orb.wait()
        owned(1 - core, theirs)

    with jax.named_scope("barrier"):
        pl.semaphore_wait(barrier, 2 * len(steps) + 1)

    with jax.named_scope("sibstart"):
        for n, e in enumerate(steps + [0]):
            for f in flavours:
                line = (first_at[f] + e) % side
                remote(theirs.at[f, line], from_sib.at[n, f], sib_send, sib_recv.at[n], sibling).start()
        to_sibling = remote(phi.at[core], phi.at[core], orb_send, orb_recv, sibling)
        to_sibling.start()
    with jax.named_scope("minepicks"):
        owned(core, mine)

    for n, e in enumerate(steps + [0]):
        with jax.named_scope("sibling%d" % n):
            wait_all(from_sib.at[n], sib_recv.at[n])
        with jax.named_scope("first%d" % n):
            for f in flavours:
                line = (first_at[f] + e) % side
                part[n, f] = mine[f, line] + from_sib[n, f]
                if e:
                    remote(
                        part.at[n, f], first_in.at[f, n], p_send.at[0], first_recv.at[f], along_first(f, e)
                    ).start()

    with jax.named_scope("tables"):
        high, low = split(cas_table())
        wide[0:SIDE, 0:SIDE] = high
        wide[0:SIDE, SIDE:] = low
        wide[SIDE:, 0:SIDE] = high
        wide[SIDE:, SIDE:] = low
        tall[0:SIDE, 0:SIDE] = high
        tall[0:SIDE, SIDE:] = high
        tall[SIDE:, 0:SIDE] = low
        tall[SIDE:, SIDE:] = low
        kern[...] = screen_kernel()

    own_line = len(steps)
    for f in flavours:
        with jax.named_scope("firstwait%d" % f):
            wait_all(first_in.at[f], first_recv.at[f])
        with jax.named_scope("second%d" % f):
            value = part[own_line, f]
            for n in range(len(steps)):
                value = value + first_in[f, n]
            summed[f] = value
            for n, e in enumerate(steps):
                remote(
                    summed.at[f], second_in.at[f, n], p_send.at[1], second_recv.at[f], along_second(f, e)
                ).start()
    for f in flavours:
        with jax.named_scope("secondwait%d" % f):
            wait_all(second_in.at[f], second_recv.at[f])
        with jax.named_scope("third%d" % f):
            value = summed[f]
            for n in range(len(steps)):
                value = value + second_in[f, n]
            line = first_at[f]
            vectors[f, line] = value
            for e in steps:
                remote(
                    vectors.at[f, line], vectors.at[f, line], p_send.at[2], third_recv.at[f], along_first(f, e)
                ).start()

    def back_copies(d):
        dy, dx = offs[d]
        to = device(at(dy, dx))
        here = dx * side + (my_y + dy) % side
        g = d // ROW_GROUP
        first = remote(quant.at[here], quant_in.at[d], q_send, q_recv.at[g], to)
        second = remote(scale.at[here], scale_in.at[d], s_send, s_recv.at[g], to)
        return first, second

    diagonal = lax.broadcasted_iota(jnp.int32, (points, SIDE), 0) == lax.broadcasted_iota(
        jnp.int32, (points, SIDE), 1
    )

    with jax.named_scope("gather"):
        to_sibling.wait()
        for f in flavours:
            wait_all(first_in.at[f], third_recv.at[f])

    for group in COLUMN_GROUPS:
        with jax.named_scope("pairs%d" % group[0]):
            size = len(group) * side
            lines = [(my_x + r) % side for r in group]
            low_half = jnp.concatenate([vectors[0, c].reshape(side * points, half) for c in lines], axis=0)
            high_half = jnp.concatenate([vectors[1, y, c] for c in lines for y in range(side)], axis=0)
            block = jnp.concatenate([low_half, high_half], axis=1)
            pair = jnp.concatenate(
                [jnp.dot(block, phi[h], preferred_element_type=F32) for h in range(2)], axis=1
            )
            peak = jnp.maximum(jnp.max(jnp.abs(pair), axis=1, keepdims=True), FLOOR)
            coded = jnp.round(pair * (TOP / peak)).astype(jnp.int32).astype(jnp.int16)
            step = jnp.broadcast_to(peak * (1.0 / TOP), (size * points, SIDE))
            for n, r in enumerate(group):
                for y in range(side):
                    rows = slice((n * side + y) * points, (n * side + y + 1) * points)
                    quant[r * side + y] = coded[rows]
                    scale[r * side + y] = jnp.sum(jnp.where(diagonal, step[rows], 0.0), axis=0, keepdims=True)
            for d in range(count):
                if offs[d][1] in group:
                    for copy in back_copies(d):
                        copy.start()

    rows = 2 * cells // SIDE

    def along(blocks):
        stacks = []
        for block, row_of, _ in blocks:
            step = jnp.sum(
                jnp.where(diagonal, jnp.broadcast_to(row_of, (points, SIDE)), 0.0), axis=1, keepdims=True
            )
            pair = block.astype(jnp.int32).astype(F32) * step
            square = pair * pair
            stacks.extend(square[:, r * SIDE : (r + 1) * SIDE] for r in range(rows))
        high, low = split(jnp.concatenate(stacks, axis=0))
        product = jnp.dot(jnp.concatenate([high, low], axis=1), wide[...], preferred_element_type=F32)
        product = product[:, :SIDE] + product[:, SIDE:]
        size = rows * points
        for n, (_, _, source) in enumerate(blocks):
            rows_done[pl.ds(pl.multiple_of(source * size, size), size), :] = product[n * size : (n + 1) * size]

    for g, start in enumerate(range(0, chips, ROW_GROUP)):
        size = min(ROW_GROUP, chips - start)
        with jax.named_scope("wait%d" % start):
            here = pl.ds(start, min(size, count - start))
            wait_all(quant_in.at[here], q_recv.at[g])
            wait_all(scale_in.at[here], s_recv.at[g])
        with jax.named_scope("along%d" % start):
            along([
                (quant_in[s], scale_in[s], at(-offs[s][0], -offs[s][1]))
                if s < count
                else (quant[my_y], scale[my_y], chip)
                for s in range(start, start + size)
            ])

    with jax.named_scope("across"):
        weight = jnp.concatenate([kern[...], kern[...]], axis=1)
        for first in range(0, points, 2):
            pieces = [rows_done[pl.ds(p, SIDE, stride=points), :] for p in (first, first + 1)]
            high, low = split(jnp.concatenate(pieces, axis=1))
            product = jnp.dot(tall[...], jnp.concatenate([high, low], axis=0), preferred_element_type=F32)
            high, low = split((product[:SIDE] + product[SIDE:]) * weight)
            middle[first // 2, 0:SIDE] = high
            middle[first // 2, SIDE:] = low
    with jax.named_scope("inverse"):
        for first in range(0, points, 2):
            product = jnp.dot(tall[...], middle[first // 2], preferred_element_type=F32)
            high, low = split(product[:SIDE] + product[SIDE:])
            for p in range(2):
                lanes = slice(p * SIDE, (p + 1) * SIDE)
                last[first + p, :, 0:SIDE] = high[:, lanes]
                last[first + p, :, SIDE:] = low[:, lanes]
    with jax.named_scope("output"):
        for first in range(0, points, 2):
            product = jnp.dot(
                last[first : first + 2].reshape(2 * SIDE, 2 * SIDE), wide[...], preferred_element_type=F32
            )
            out_ref[first : first + 2] = (product[:, :SIDE] + product[:, SIDE:]).reshape(2, SIDE, SIDE)

    with jax.named_scope("sends"):
        wait_all(from_sib, sib_send)
        for n in range(3):
            wait_all(first_in, p_send.at[n])
        wait_all(quant_in, q_send)
        wait_all(scale_in, s_send)


def shards(side, orbitals, point_index):
    orbital_count, cells = orbitals.shape
    chips = side * side
    points = point_index.shape[0] // (2 * chips)
    others = chips - 1
    half = orbital_count // 2
    dma = pltpu.SemaphoreType.DMA
    in_place = functools.partial(pltpu.with_memory_space_constraint, memory_space=pltpu.HBM)
    row_groups = pl.cdiv(chips, ROW_GROUP)
    out = pl.pallas_call(
        functools.partial(body, side, points),
        out_shape=jax.ShapeDtypeStruct((points, SIDE, SIDE), F32),
        in_specs=[pl.BlockSpec(memory_space=pltpu.HBM)] * 2,
        out_specs=pl.BlockSpec(memory_space=pltpu.VMEM),
        scratch_shapes=[
            pltpu.VMEM((2, orbital_count, cells), BF16),
            pltpu.VMEM((1, point_index.shape[0]), jnp.int32),
            pltpu.VMEM((2, side, side, points, half), BF16),
            pltpu.VMEM((2, side, side, points, half), BF16),
            pltpu.VMEM((side, 2, side, points, half), BF16),
            pltpu.VMEM((side, 2, side, points, half), BF16),
            pltpu.VMEM((2, side - 1, side, points, half), BF16),
            pltpu.VMEM((2, side, points, half), BF16),
            pltpu.VMEM((2, side - 1, side, points, half), BF16),
            pltpu.VMEM((2, side, side, points, half), BF16),
            pltpu.VMEM((chips, points, 2 * cells), jnp.int16),
            pltpu.VMEM((chips, 1, SIDE), F32),
            pltpu.VMEM((others, points, 2 * cells), jnp.int16),
            pltpu.VMEM((others, 1, SIDE), F32),
            pltpu.VMEM((SIDE * points, SIDE), F32),
            pltpu.VMEM((2 * SIDE, 2 * SIDE), BF16),
            pltpu.VMEM((2 * SIDE, 2 * SIDE), BF16),
            pltpu.VMEM((SIDE, SIDE), F32),
            pltpu.VMEM((points // 2, 2 * SIDE, 2 * SIDE), BF16),
            pltpu.VMEM((points, SIDE, 2 * SIDE), BF16),
            dma((2,)), dma, dma((side,)), dma, dma,
            dma((3,)), dma((2,)), dma((2,)), dma((2,)),
            dma, dma((row_groups,)), dma, dma((row_groups,)),
        ],
        compiler_params=pltpu.CompilerParams(
            collective_id=0, has_side_effects=True, vmem_limit_bytes=VMEM_BYTES
        ),
    )(in_place(orbitals), in_place(point_index.reshape(1, -1)))
    return out[None]


def solution(mesh):
    grid_count = mesh.shape["grid"]
    size = math.isqrt(grid_count // 2)
    in_specs = (P(None, "grid"), P("pts"))
    out_specs = P("pts", "grid", None, None)
    step = functools.partial(shards, size)
    return jax.shard_map(step, mesh=mesh, in_specs=in_specs, out_specs=out_specs, check_vma=False)
```

time: 33 us -> 32 us (0.970)
  Pallas kernels: 31.9 us -> 30.9 us
    pallas_call x1, Pallas kernels: 31.9 us -> 30.9 us  [shards(): pl.pallas_call(functools.partial(body, side, points), out_shape=jax.Shape...]
where the time goes in v3:
time: 32 us; the launch traced here: 31.9 us
  Pallas kernels  30.9 us (97%)
  local copies, waits for them, and re-layouts  0.97 us (3%)
    pallas_call x1, Pallas kernels, shards(): pl.pallas_call(functools.partial(body, side, points), out_shape=jax.Shape...  30.9 us
    unnamed x1, local copies, waits for them, and re-layouts  0.97 us

profile of v3, /device:TPU:1, one launch (start us, length us, event | category | flops | bytes accessed | tf_op | source)
XLA Modules:
  0.0 31.9 jit_solution(4987303992769801496)
XLA Ops:
  0.0 30.9 %shard_map.28 = f32[16,128,128]{2,1,0:T(8,128)S(1)} custom-call(bf16[512,512]{1,0:T(8,128)(2,1)} %orb_hbm.1, s32[1,512]{1,0:T(1,128)} %bitcast.3), custom_call_target="tpu_custom_call" | custom-call | tf_op jit(solution)/shard_map/pallas_call | solution.py:308
  30.9 1.0 %copy.4 = f32[1,16,128,128]{3,2,1,0:T(8,128)} copy(f32[1,16,128,128]{3,2,1,0:T(8,128)S(1)} %bitcast.2) | data formatting | bytes 2097152

commit v4 on v3

--- a/solution.py
+++ b/solution.py
@@ -14,8 +14,8 @@
 BF16 = jnp.bfloat16
 TOP = 32766.0
 FLOOR = 1e-30
-COLUMN_GROUPS = ((2, 1), (3, 0))
-ROW_GROUP = 4
+COLUMN_GROUPS = ((2, 1, 3, 0),)
+ROW_GROUP = 8
 VMEM_BYTES = 16 * 1024 * 1024
 
 
@@ -49,9 +49,9 @@
 
 def body(
     side, points,
-    orb_hbm, idx_hbm, out_ref,
+    orb_hbm, idx_hbm, last, wide,
     phi, idx, mine, theirs, from_sib, part, first_in, summed, second_in, vectors, quant, scale, quant_in, scale_in,
-    rows_done, wide, tall, kern, middle, last,
+    rows_done, tall, kern, middle,
     load_sem, sib_send, sib_recv, orb_send, orb_recv, p_send, first_recv, second_recv, third_recv,
     q_send, q_recv, s_send, s_recv,
 ):
@@ -281,19 +281,22 @@
                 lanes = slice(p * SIDE, (p + 1) * SIDE)
                 last[first + p, :, 0:SIDE] = high[:, lanes]
                 last[first + p, :, SIDE:] = low[:, lanes]
-    with jax.named_scope("output"):
-        for first in range(0, points, 2):
-            product = jnp.dot(
-                last[first : first + 2].reshape(2 * SIDE, 2 * SIDE), wide[...], preferred_element_type=F32
-            )
-            out_ref[first : first + 2] = (product[:, :SIDE] + product[:, SIDE:]).reshape(2, SIDE, SIDE)
-
     with jax.named_scope("sends"):
         wait_all(from_sib, sib_send)
         for n in range(3):
             wait_all(first_in, p_send.at[n])
         wait_all(quant_in, q_send)
         wait_all(scale_in, s_send)
+
+
+def finish(last, wide, out_hbm, sheets, sem):
+    points = last.shape[0]
+    for first in range(0, points, 2):
+        pair = pl.ds(first, 2)
+        product = jnp.dot(last[pair].reshape(2 * SIDE, 2 * SIDE), wide[...], preferred_element_type=F32)
+        sheets[pair] = (product[:, :SIDE] + product[:, SIDE:]).reshape(2, SIDE, SIDE)
+        pltpu.make_async_copy(sheets.at[pair], out_hbm.at[pair], sem).start()
+    pltpu.make_async_copy(sheets, out_hbm, sem).wait()
 
 
 def shards(side, orbitals, point_index):
@@ -305,11 +308,14 @@
     dma = pltpu.SemaphoreType.DMA
     in_place = functools.partial(pltpu.with_memory_space_constraint, memory_space=pltpu.HBM)
     row_groups = pl.cdiv(chips, ROW_GROUP)
-    out = pl.pallas_call(
+    last, wide = pl.pallas_call(
         functools.partial(body, side, points),
-        out_shape=jax.ShapeDtypeStruct((points, SIDE, SIDE), F32),
+        out_shape=[
+            jax.ShapeDtypeStruct((points, SIDE, 2 * SIDE), BF16),
+            jax.ShapeDtypeStruct((2 * SIDE, 2 * SIDE), BF16),
+        ],
         in_specs=[pl.BlockSpec(memory_space=pltpu.HBM)] * 2,
-        out_specs=pl.BlockSpec(memory_space=pltpu.VMEM),
+        out_specs=[pl.BlockSpec(memory_space=pltpu.VMEM)] * 2,
         scratch_shapes=[
             pltpu.VMEM((2, orbital_count, cells), BF16),
             pltpu.VMEM((1, point_index.shape[0]), jnp.int32),
@@ -327,10 +333,8 @@
             pltpu.VMEM((others, 1, SIDE), F32),
             pltpu.VMEM((SIDE * points, SIDE), F32),
             pltpu.VMEM((2 * SIDE, 2 * SIDE), BF16),
-            pltpu.VMEM((2 * SIDE, 2 * SIDE), BF16),
             pltpu.VMEM((SIDE, SIDE), F32),
             pltpu.VMEM((points // 2, 2 * SIDE, 2 * SIDE), BF16),
-            pltpu.VMEM((points, SIDE, 2 * SIDE), BF16),
             dma((2,)), dma, dma((side,)), dma, dma,
             dma((3,)), dma((2,)), dma((2,)), dma((2,)),
             dma, dma((row_groups,)), dma, dma((row_groups,)),
@@ -339,6 +343,14 @@
             collective_id=0, has_side_effects=True, vmem_limit_bytes=VMEM_BYTES
         ),
     )(in_place(orbitals), in_place(point_index.reshape(1, -1)))
+    out = pl.pallas_call(
+        finish,
+        out_shape=jax.ShapeDtypeStruct((points, SIDE, SIDE), F32),
+        in_specs=[pl.BlockSpec(memory_space=pltpu.VMEM)] * 2,
+        out_specs=pl.BlockSpec(memory_space=pltpu.HBM),
+        scratch_shapes=[pltpu.VMEM((points, SIDE, SIDE), F32), dma],
+        compiler_params=pltpu.CompilerParams(vmem_limit_bytes=8 * 1024 * 1024),
+    )(last, wide)
     return out[None]
 
 

time: 32 us -> 31.4 us (0.981)
  local copies, waits for them, and re-layouts: 0.97 us -> 0 us
    unnamed x1 -> x0, local copies, waits for them, and re-layouts: 0.97 us -> none
    pallas_call x1 -> x2, Pallas kernels: 30.9 us -> 31.2 us  [the longest x1 30 us: shards(): pl.pallas_call(functools.partial(body, side, points), out_shape=[jax.Shap...]
where the time goes in v4:
time: 31.4 us; the launch traced here: 31.2 us
  Pallas kernels  31.2 us (99%)
    pallas_call x1, Pallas kernels, shards(): pl.pallas_call(functools.partial(body, side, points), out_shape=[jax.Shap...  30 us
    pallas_call x1, Pallas kernels, shards(): pl.pallas_call(finish, out_shape=jax.ShapeDtypeStruct((points, SIDE, SIDE...  1.2 us

profile of v4, /device:TPU:1, one launch (start us, length us, event | category | flops | bytes accessed | tf_op | source)
XLA Modules:
  0.0 31.2 jit_solution(4589746655762074889)
XLA Ops:
  0.0 30.0 %shard_map.28 = (bf16[16,128,256]{2,1,0:T(8,128)(2,1)S(1)}, bf16[256,256]{1,0:T(8,128)(2,1)S(1)}) custom-call(bf16[512,512]{1,0:T(8,128)(2,1)} %orb_hbm.1, s32[1,512]{1,0:T(1,128)} %bitcast.2), custom_call_target="tpu_custom_call" | custom-call | tf_op jit(solution)/shard_map/pallas_call | solution.py:311
  30.0 1.2 %shard_map.29 = f32[16,128,128]{2,1,0:T(8,128)} custom-call(bf16[16,128,256]{2,1,0:T(8,128)(2,1)S(1)} %get-tuple-element.7.last, bf16[256,256]{1,0:T(8,128)(2,1)S(1)} %get-tuple-element.8.wide), custom_call_target="tpu_custom_call" | custom-call | tf_op jit(solution)/shard_map/pallas_call | solution.py:346

commit v5 on v4

--- a/solution.py
+++ b/solution.py
@@ -14,8 +14,7 @@
 BF16 = jnp.bfloat16
 TOP = 32766.0
 FLOOR = 1e-30
-COLUMN_GROUPS = ((2, 1, 3, 0),)
-ROW_GROUP = 8
+REST_GROUPS = (6, 6)
 VMEM_BYTES = 16 * 1024 * 1024
 
 
@@ -63,12 +62,13 @@
     chips = side * side
     cells = phi.shape[2]
     orbital_count = phi.shape[1]
-    half = orbital_count // 2
+    part_points = points // 2
     offs = offsets(side, side)
     count = len(offs)
     steps = [2, 1, 3][-(side - 1) :]
     flavours = range(2)
     first_at = (my_x, my_y)
+    second_at = (my_y, my_x)
 
     def at(dy, dx):
         return ((my_y + dy + side) % side) * side + (my_x + dx + side) % side
@@ -116,12 +116,11 @@
             [jnp.where(chosen == lane + j * SIDE, 1.0, 0.0).astype(BF16) for j in range(cells // SIDE)], axis=1
         )
         found = lax.dot_general(mask, phi[core], (((1,), (1,)), ((), ())), preferred_element_type=F32)
-        found = found.astype(BF16)
         for y in range(side):
             for x in range(side):
-                rows = slice((y * side + x) * points, (y * side + x + 1) * points)
-                to[0, x, y] = found[rows, :half]
-                to[1, y, x] = found[rows, half:]
+                at_row = (y * side + x) * points
+                to[0, x, y] = found[at_row : at_row + part_points].astype(BF16)
+                to[1, y, x] = found[at_row + part_points : at_row + points].astype(BF16)
 
     with jax.named_scope("ownpicks"):
         load_orb.wait()
@@ -191,54 +190,63 @@
                     vectors.at[f, line], vectors.at[f, line], p_send.at[2], third_recv.at[f], along_first(f, e)
                 ).start()
 
-    def back_copies(d):
-        dy, dx = offs[d]
-        to = device(at(dy, dx))
-        here = dx * side + (my_y + dy) % side
-        g = d // ROW_GROUP
-        first = remote(quant.at[here], quant_in.at[d], q_send, q_recv.at[g], to)
-        second = remote(scale.at[here], scale_in.at[d], s_send, s_recv.at[g], to)
-        return first, second
-
-    diagonal = lax.broadcasted_iota(jnp.int32, (points, SIDE), 0) == lax.broadcasted_iota(
-        jnp.int32, (points, SIDE), 1
+    slots = [
+        [o for o in offs if o[1 - f] == 0] + [o for o in offs if o[1 - f] != 0] for f in flavours
+    ]
+    sizes = (len(steps),) + REST_GROUPS
+    bounds = [sum(sizes[:g]) for g in range(len(sizes) + 1)]
+
+    def back_copies(f, g):
+        copies = []
+        for n in range(bounds[g], bounds[g + 1]):
+            dy, dx = slots[f][n]
+            line, place = ((dx, (my_y + dy) % side), (dy, (my_x + dx) % side))[f]
+            to = device(at(dy, dx))
+            copies.append(remote(scale.at[f, line, place], scale_in.at[f, n], s_send, s_recv.at[f, g], to))
+            copies.append(remote(quant.at[f, line, place], quant_in.at[f, n], q_send, q_recv.at[f, g], to))
+        return copies
+
+    diagonal = lax.broadcasted_iota(jnp.int32, (part_points, SIDE), 0) == lax.broadcasted_iota(
+        jnp.int32, (part_points, SIDE), 1
     )
 
-    with jax.named_scope("gather"):
-        to_sibling.wait()
-        for f in flavours:
+    def pairs(f, lines):
+        size = len(lines) * side * part_points
+        block = jnp.concatenate(
+            [vectors[f, (first_at[f] + r) % side].reshape(side * part_points, orbital_count) for r in lines], axis=0
+        )
+        pair = jnp.concatenate([jnp.dot(block, phi[h], preferred_element_type=F32) for h in range(2)], axis=1)
+        peak = jnp.maximum(jnp.max(jnp.abs(pair), axis=1, keepdims=True), FLOOR)
+        coded = jnp.round(pair * (TOP / peak)).astype(jnp.int32)
+        step = jnp.broadcast_to(peak * (1.0 / TOP), (size, SIDE))
+        for n, r in enumerate(lines):
+            for place in range(side):
+                rows = slice((n * side + place) * part_points, (n * side + place + 1) * part_points)
+                quant[f, r, place] = coded[rows].astype(jnp.int16)
+                scale[f, r, place] = jnp.sum(jnp.where(diagonal, step[rows], 0.0), axis=0, keepdims=True)
+
+    to_sibling.wait()
+    for f in flavours:
+        with jax.named_scope("early%d" % f):
+            pairs(f, [0])
+            for copy in back_copies(f, 0):
+                copy.start()
+    for f in flavours:
+        with jax.named_scope("gather%d" % f):
             wait_all(first_in.at[f], third_recv.at[f])
-
-    for group in COLUMN_GROUPS:
-        with jax.named_scope("pairs%d" % group[0]):
-            size = len(group) * side
-            lines = [(my_x + r) % side for r in group]
-            low_half = jnp.concatenate([vectors[0, c].reshape(side * points, half) for c in lines], axis=0)
-            high_half = jnp.concatenate([vectors[1, y, c] for c in lines for y in range(side)], axis=0)
-            block = jnp.concatenate([low_half, high_half], axis=1)
-            pair = jnp.concatenate(
-                [jnp.dot(block, phi[h], preferred_element_type=F32) for h in range(2)], axis=1
-            )
-            peak = jnp.maximum(jnp.max(jnp.abs(pair), axis=1, keepdims=True), FLOOR)
-            coded = jnp.round(pair * (TOP / peak)).astype(jnp.int32).astype(jnp.int16)
-            step = jnp.broadcast_to(peak * (1.0 / TOP), (size * points, SIDE))
-            for n, r in enumerate(group):
-                for y in range(side):
-                    rows = slice((n * side + y) * points, (n * side + y + 1) * points)
-                    quant[r * side + y] = coded[rows]
-                    scale[r * side + y] = jnp.sum(jnp.where(diagonal, step[rows], 0.0), axis=0, keepdims=True)
-            for d in range(count):
-                if offs[d][1] in group:
-                    for copy in back_copies(d):
-                        copy.start()
+        with jax.named_scope("pairs%d" % f):
+            pairs(f, steps)
+            for g in range(1, len(sizes)):
+                for copy in back_copies(f, g):
+                    copy.start()
 
     rows = 2 * cells // SIDE
 
-    def along(blocks):
+    def along(f, blocks):
         stacks = []
         for block, row_of, _ in blocks:
             step = jnp.sum(
-                jnp.where(diagonal, jnp.broadcast_to(row_of, (points, SIDE)), 0.0), axis=1, keepdims=True
+                jnp.where(diagonal, jnp.broadcast_to(row_of, (part_points, SIDE)), 0.0), axis=1, keepdims=True
             )
             pair = block.astype(jnp.int32).astype(F32) * step
             square = pair * pair
@@ -246,28 +254,30 @@
         high, low = split(jnp.concatenate(stacks, axis=0))
         product = jnp.dot(jnp.concatenate([high, low], axis=1), wide[...], preferred_element_type=F32)
         product = product[:, :SIDE] + product[:, SIDE:]
-        size = rows * points
+        size = rows * part_points
         for n, (_, _, source) in enumerate(blocks):
-            rows_done[pl.ds(pl.multiple_of(source * size, size), size), :] = product[n * size : (n + 1) * size]
-
-    for g, start in enumerate(range(0, chips, ROW_GROUP)):
-        size = min(ROW_GROUP, chips - start)
-        with jax.named_scope("wait%d" % start):
-            here = pl.ds(start, min(size, count - start))
-            wait_all(quant_in.at[here], q_recv.at[g])
-            wait_all(scale_in.at[here], s_recv.at[g])
-        with jax.named_scope("along%d" % start):
-            along([
-                (quant_in[s], scale_in[s], at(-offs[s][0], -offs[s][1]))
-                if s < count
-                else (quant[my_y], scale[my_y], chip)
-                for s in range(start, start + size)
-            ])
+            rows_done[f, pl.ds(pl.multiple_of(source * size, size), size), :] = product[n * size : (n + 1) * size]
+
+    for f, g in [(0, 0), (1, 0)] + [(f, g) for f in flavours for g in range(1, len(sizes))]:
+        group = range(bounds[g], bounds[g + 1])
+        with jax.named_scope("wait%d%d" % (f, g)):
+            wait_all(quant_in.at[f, pl.ds(bounds[g], sizes[g])], q_recv.at[f, g])
+            wait_all(scale_in.at[f, pl.ds(bounds[g], sizes[g])], s_recv.at[f, g])
+        with jax.named_scope("along%d%d" % (f, g)):
+            blocks = [
+                (quant_in[f, n], scale_in[f, n], at(-slots[f][n][0], -slots[f][n][1])) for n in group
+            ]
+            if g == 0:
+                blocks.append((quant[f, 0, second_at[f]], scale[f, 0, second_at[f]], chip))
+            along(f, blocks)
 
     with jax.named_scope("across"):
         weight = jnp.concatenate([kern[...], kern[...]], axis=1)
         for first in range(0, points, 2):
-            pieces = [rows_done[pl.ds(p, SIDE, stride=points), :] for p in (first, first + 1)]
+            pieces = [
+                rows_done[p // part_points, pl.ds(p % part_points, SIDE, stride=part_points), :]
+                for p in (first, first + 1)
+            ]
             high, low = split(jnp.concatenate(pieces, axis=1))
             product = jnp.dot(tall[...], jnp.concatenate([high, low], axis=0), preferred_element_type=F32)
             high, low = split((product[:SIDE] + product[SIDE:]) * weight)
@@ -304,10 +314,10 @@
     chips = side * side
     points = point_index.shape[0] // (2 * chips)
     others = chips - 1
-    half = orbital_count // 2
+    part_points = points // 2
     dma = pltpu.SemaphoreType.DMA
     in_place = functools.partial(pltpu.with_memory_space_constraint, memory_space=pltpu.HBM)
-    row_groups = pl.cdiv(chips, ROW_GROUP)
+    groups = 1 + len(REST_GROUPS)
     last, wide = pl.pallas_call(
         functools.partial(body, side, points),
         out_shape=[
@@ -319,25 +329,25 @@
         scratch_shapes=[
             pltpu.VMEM((2, orbital_count, cells), BF16),
             pltpu.VMEM((1, point_index.shape[0]), jnp.int32),
-            pltpu.VMEM((2, side, side, points, half), BF16),
-            pltpu.VMEM((2, side, side, points, half), BF16),
-            pltpu.VMEM((side, 2, side, points, half), BF16),
-            pltpu.VMEM((side, 2, side, points, half), BF16),
-            pltpu.VMEM((2, side - 1, side, points, half), BF16),
-            pltpu.VMEM((2, side, points, half), BF16),
-            pltpu.VMEM((2, side - 1, side, points, half), BF16),
-            pltpu.VMEM((2, side, side, points, half), BF16),
-            pltpu.VMEM((chips, points, 2 * cells), jnp.int16),
-            pltpu.VMEM((chips, 1, SIDE), F32),
-            pltpu.VMEM((others, points, 2 * cells), jnp.int16),
-            pltpu.VMEM((others, 1, SIDE), F32),
-            pltpu.VMEM((SIDE * points, SIDE), F32),
+            pltpu.VMEM((2, side, side, part_points, orbital_count), BF16),
+            pltpu.VMEM((2, side, side, part_points, orbital_count), BF16),
+            pltpu.VMEM((side, 2, side, part_points, orbital_count), BF16),
+            pltpu.VMEM((side, 2, side, part_points, orbital_count), BF16),
+            pltpu.VMEM((2, side - 1, side, part_points, orbital_count), BF16),
+            pltpu.VMEM((2, side, part_points, orbital_count), BF16),
+            pltpu.VMEM((2, side - 1, side, part_points, orbital_count), BF16),
+            pltpu.VMEM((2, side, side, part_points, orbital_count), BF16),
+            pltpu.VMEM((2, side, side, part_points, 2 * cells), jnp.int16),
+            pltpu.VMEM((2, side, side, 1, SIDE), F32),
+            pltpu.VMEM((2, others, part_points, 2 * cells), jnp.int16),
+            pltpu.VMEM((2, others, 1, SIDE), F32),
+            pltpu.VMEM((2, SIDE * part_points, SIDE), F32),
             pltpu.VMEM((2 * SIDE, 2 * SIDE), BF16),
             pltpu.VMEM((SIDE, SIDE), F32),
             pltpu.VMEM((points // 2, 2 * SIDE, 2 * SIDE), BF16),
             dma((2,)), dma, dma((side,)), dma, dma,
             dma((3,)), dma((2,)), dma((2,)), dma((2,)),
-            dma, dma((row_groups,)), dma, dma((row_groups,)),
+            dma, dma((2, groups)), dma, dma((2, groups)),
         ],
         compiler_params=pltpu.CompilerParams(
             collective_id=0, has_side_effects=True, vmem_limit_bytes=VMEM_BYTES

time: 31.4 us -> 29.6 us (0.943)
  Pallas kernels: 31.2 us -> 29.4 us
    pallas_call x1, Pallas kernels: 30 us -> 28.2 us  [shards(): pl.pallas_call(functools.partial(body, side, points), out_shape=[jax.Shap...]
where the time goes in v5:
time: 29.6 us; the launch traced here: 29.4 us
  Pallas kernels  29.4 us (99%)
    pallas_call x1, Pallas kernels, shards(): pl.pallas_call(functools.partial(body, side, points), out_shape=[jax.Shap...  28.2 us
    pallas_call x1, Pallas kernels, shards(): pl.pallas_call(finish, out_shape=jax.ShapeDtypeStruct((points, SIDE, SIDE...  1.2 us

profile of v5, /device:TPU:1, one launch (start us, length us, event | category | flops | bytes accessed | tf_op | source)
XLA Modules:
  0.0 29.4 jit_solution(1414038607573859028)
XLA Ops:
  0.0 28.2 %shard_map.28 = (bf16[16,128,256]{2,1,0:T(8,128)(2,1)S(1)}, bf16[256,256]{1,0:T(8,128)(2,1)S(1)}) custom-call(bf16[512,512]{1,0:T(8,128)(2,1)} %orb_hbm.1, s32[1,512]{1,0:T(1,128)} %bitcast.2), custom_call_target="tpu_custom_call" | custom-call | tf_op jit(solution)/shard_map/pallas_call | solution.py:321
  28.2 1.2 %shard_map.29 = f32[16,128,128]{2,1,0:T(8,128)} custom-call(bf16[16,128,256]{2,1,0:T(8,128)(2,1)S(1)} %get-tuple-element.7.last, bf16[256,256]{1,0:T(8,128)(2,1)S(1)} %get-tuple-element.8.wide), custom_call_target="tpu_custom_call" | custom-call | tf_op jit(solution)/shard_map/pallas_call | solution.py:356

commit v6 on v5

--- a/solution.py
+++ b/solution.py
@@ -14,7 +14,7 @@
 BF16 = jnp.bfloat16
 TOP = 32766.0
 FLOOR = 1e-30
-REST_GROUPS = (6, 6)
+REST_GROUPS = (12,)
 VMEM_BYTES = 16 * 1024 * 1024
 
 
@@ -48,9 +48,9 @@
 
 def body(
     side, points,
-    orb_hbm, idx_hbm, last, wide,
-    phi, idx, mine, theirs, from_sib, part, first_in, summed, second_in, vectors, quant, scale, quant_in, scale_in,
-    rows_done, tall, kern, middle,
+    orb_hbm, idx_hbm, done, last, wide,
+    phi, idx, their_mask, mine, theirs, from_sib, part, first_in, summed, second_in, vectors, quant, scale, quant_in, scale_in,
+    rows_done, tall, kern, middle, first_last,
     load_sem, sib_send, sib_recv, orb_send, orb_recv, p_send, first_recv, second_recv, third_recv,
     q_send, q_recv, s_send, s_recv,
 ):
@@ -110,11 +110,13 @@
         column = column.reshape(chips, 2, points, SIDE)
         lane = lax.broadcasted_iota(jnp.int32, (chips * points, SIDE), 1)
 
-    def owned(layer, to):
+    def mask_of(layer):
         chosen = jnp.where(layer == 0, column[:, 0], column[:, 1]).reshape(chips * points, SIDE)
-        mask = jnp.concatenate(
+        return jnp.concatenate(
             [jnp.where(chosen == lane + j * SIDE, 1.0, 0.0).astype(BF16) for j in range(cells // SIDE)], axis=1
         )
+
+    def owned(mask, to):
         found = lax.dot_general(mask, phi[core], (((1,), (1,)), ((), ())), preferred_element_type=F32)
         for y in range(side):
             for x in range(side):
@@ -123,8 +125,9 @@
                 to[1, y, x] = found[at_row + part_points : at_row + points].astype(BF16)
 
     with jax.named_scope("ownpicks"):
+        their_mask[...] = mask_of(1 - core)
         load_orb.wait()
-        owned(1 - core, theirs)
+        owned(their_mask[...], theirs)
 
     with jax.named_scope("barrier"):
         pl.semaphore_wait(barrier, 2 * len(steps) + 1)
@@ -137,7 +140,7 @@
         to_sibling = remote(phi.at[core], phi.at[core], orb_send, orb_recv, sibling)
         to_sibling.start()
     with jax.named_scope("minepicks"):
-        owned(core, mine)
+        owned(mask_of(core), mine)
 
     for n, e in enumerate(steps + [0]):
         with jax.named_scope("sibling%d" % n):
@@ -258,6 +261,24 @@
         for n, (_, _, source) in enumerate(blocks):
             rows_done[f, pl.ds(pl.multiple_of(source * size, size), size), :] = product[n * size : (n + 1) * size]
 
+    def across(f):
+        weight = jnp.concatenate([kern[...], kern[...]], axis=1)
+        for n in range(part_points // 2):
+            pieces = [rows_done[f, pl.ds(p, SIDE, stride=part_points), :] for p in (2 * n, 2 * n + 1)]
+            high, low = split(jnp.concatenate(pieces, axis=1))
+            product = jnp.dot(tall[...], jnp.concatenate([high, low], axis=0), preferred_element_type=F32)
+            high, low = split((product[:SIDE] + product[SIDE:]) * weight)
+            middle[f, n, 0:SIDE] = high
+            middle[f, n, SIDE:] = low
+        for n in range(part_points // 2):
+            product = jnp.dot(tall[...], middle[f, n], preferred_element_type=F32)
+            high, low = split(product[:SIDE] + product[SIDE:])
+            for p in range(2):
+                lanes = slice(p * SIDE, (p + 1) * SIDE)
+                to = (first_last, last)[f]
+                to[2 * n + p, :, 0:SIDE] = high[:, lanes]
+                to[2 * n + p, :, SIDE:] = low[:, lanes]
+
     for f, g in [(0, 0), (1, 0)] + [(f, g) for f in flavours for g in range(1, len(sizes))]:
         group = range(bounds[g], bounds[g + 1])
         with jax.named_scope("wait%d%d" % (f, g)):
@@ -270,27 +291,14 @@
             if g == 0:
                 blocks.append((quant[f, 0, second_at[f]], scale[f, 0, second_at[f]], chip))
             along(f, blocks)
-
-    with jax.named_scope("across"):
-        weight = jnp.concatenate([kern[...], kern[...]], axis=1)
-        for first in range(0, points, 2):
-            pieces = [
-                rows_done[p // part_points, pl.ds(p % part_points, SIDE, stride=part_points), :]
-                for p in (first, first + 1)
-            ]
-            high, low = split(jnp.concatenate(pieces, axis=1))
-            product = jnp.dot(tall[...], jnp.concatenate([high, low], axis=0), preferred_element_type=F32)
-            high, low = split((product[:SIDE] + product[SIDE:]) * weight)
-            middle[first // 2, 0:SIDE] = high
-            middle[first // 2, SIDE:] = low
-    with jax.named_scope("inverse"):
-        for first in range(0, points, 2):
-            product = jnp.dot(tall[...], middle[first // 2], preferred_element_type=F32)
-            high, low = split(product[:SIDE] + product[SIDE:])
-            for p in range(2):
-                lanes = slice(p * SIDE, (p + 1) * SIDE)
-                last[first + p, :, 0:SIDE] = high[:, lanes]
-                last[first + p, :, SIDE:] = low[:, lanes]
+        if g == len(sizes) - 1:
+            with jax.named_scope("across%d" % f):
+                across(f)
+            if f == 0:
+                with jax.named_scope("output"):
+                    for first in range(0, part_points, 2):
+                        done[first : first + 2] = last_product(first_last[first : first + 2], wide[...])
+
     with jax.named_scope("sends"):
         wait_all(from_sib, sib_send)
         for n in range(3):
@@ -299,14 +307,21 @@
         wait_all(scale_in, s_send)
 
 
-def finish(last, wide, out_hbm, sheets, sem):
-    points = last.shape[0]
-    for first in range(0, points, 2):
-        pair = pl.ds(first, 2)
-        product = jnp.dot(last[pair].reshape(2 * SIDE, 2 * SIDE), wide[...], preferred_element_type=F32)
-        sheets[pair] = (product[:, :SIDE] + product[:, SIDE:]).reshape(2, SIDE, SIDE)
-        pltpu.make_async_copy(sheets.at[pair], out_hbm.at[pair], sem).start()
-    pltpu.make_async_copy(sheets, out_hbm, sem).wait()
+def last_product(values, wide):
+    count = values.shape[0]
+    product = jnp.dot(values.reshape(count * SIDE, 2 * SIDE), wide, preferred_element_type=F32)
+    return (product[:, :SIDE] + product[:, SIDE:]).reshape(count, SIDE, SIDE)
+
+
+def finish(done, last, wide, out_hbm, sheets, sem):
+    ready = done.shape[0]
+    pltpu.make_async_copy(done, out_hbm.at[pl.ds(0, ready)], sem).start()
+    for first in range(0, last.shape[0], 2):
+        sheets[first : first + 2] = last_product(last[first : first + 2], wide[...])
+        pltpu.make_async_copy(
+            sheets.at[pl.ds(first, 2)], out_hbm.at[pl.ds(ready + first, 2)], sem
+        ).start()
+    pltpu.make_async_copy(out_hbm, out_hbm, sem).wait()
 
 
 def shards(side, orbitals, point_index):
@@ -318,17 +333,19 @@
     dma = pltpu.SemaphoreType.DMA
     in_place = functools.partial(pltpu.with_memory_space_constraint, memory_space=pltpu.HBM)
     groups = 1 + len(REST_GROUPS)
-    last, wide = pl.pallas_call(
+    done, last, wide = pl.pallas_call(
         functools.partial(body, side, points),
         out_shape=[
-            jax.ShapeDtypeStruct((points, SIDE, 2 * SIDE), BF16),
+            jax.ShapeDtypeStruct((part_points, SIDE, SIDE), F32),
+            jax.ShapeDtypeStruct((part_points, SIDE, 2 * SIDE), BF16),
             jax.ShapeDtypeStruct((2 * SIDE, 2 * SIDE), BF16),
         ],
         in_specs=[pl.BlockSpec(memory_space=pltpu.HBM)] * 2,
-        out_specs=[pl.BlockSpec(memory_space=pltpu.VMEM)] * 2,
+        out_specs=[pl.BlockSpec(memory_space=pltpu.VMEM)] * 3,
         scratch_shapes=[
             pltpu.VMEM((2, orbital_count, cells), BF16),
             pltpu.VMEM((1, point_index.shape[0]), jnp.int32),
+            pltpu.VMEM((chips * points, cells), BF16),
             pltpu.VMEM((2, side, side, part_points, orbital_count), BF16),
             pltpu.VMEM((2, side, side, part_points, orbital_count), BF16),
             pltpu.VMEM((side, 2, side, part_points, orbital_count), BF16),
@@ -344,7 +361,8 @@
             pltpu.VMEM((2, SIDE * part_points, SIDE), F32),
             pltpu.VMEM((2 * SIDE, 2 * SIDE), BF16),
             pltpu.VMEM((SIDE, SIDE), F32),
-            pltpu.VMEM((points // 2, 2 * SIDE, 2 * SIDE), BF16),
+            pltpu.VMEM((2, part_points // 2, 2 * SIDE, 2 * SIDE), BF16),
+            pltpu.VMEM((part_points, SIDE, 2 * SIDE), BF16),
             dma((2,)), dma, dma((side,)), dma, dma,
             dma((3,)), dma((2,)), dma((2,)), dma((2,)),
             dma, dma((2, groups)), dma, dma((2, groups)),
@@ -356,11 +374,11 @@
     out = pl.pallas_call(
         finish,
         out_shape=jax.ShapeDtypeStruct((points, SIDE, SIDE), F32),
-        in_specs=[pl.BlockSpec(memory_space=pltpu.VMEM)] * 2,
+        in_specs=[pl.BlockSpec(memory_space=pltpu.VMEM)] * 3,
         out_specs=pl.BlockSpec(memory_space=pltpu.HBM),
-        scratch_shapes=[pltpu.VMEM((points, SIDE, SIDE), F32), dma],
+        scratch_shapes=[pltpu.VMEM((part_points, SIDE, SIDE), F32), dma],
         compiler_params=pltpu.CompilerParams(vmem_limit_bytes=8 * 1024 * 1024),
-    )(last, wide)
+    )(done, last, wide)
     return out[None]
 
 

time: 29.6 us -> 29 us (0.980)
  Pallas kernels: 29.4 us -> 28.8 us
    pallas_call x1, Pallas kernels: 28.2 us -> 27.8 us  [shards(): pl.pallas_call(functools.partial(body, side, points), out_shape=[jax.Shap...]
where the time goes in v6:
time: 29 us; the launch traced here: 28.8 us
  Pallas kernels  28.8 us (99%)
    pallas_call x1, Pallas kernels, shards(): pl.pallas_call(functools.partial(body, side, points), out_shape=[jax.Shap...  27.8 us
    pallas_call x1, Pallas kernels, shards(): pl.pallas_call(finish, out_shape=jax.ShapeDtypeStruct((points, SIDE, SIDE...  1.03 us

profile of v6, /device:TPU:1, one launch (start us, length us, event | category | flops | bytes accessed | tf_op | source)
XLA Modules:
  0.0 28.8 jit_solution(4796902330521734698)
XLA Ops:
  0.0 27.8 %shard_map.28 = (f32[8,128,128]{2,1,0:T(8,128)S(1)}, bf16[8,128,256]{2,1,0:T(8,128)(2,1)S(1)}, bf16[256,256]{1,0:T(8,128)(2,1)S(1)}) custom-call(bf16[512,512]{1,0:T(8,128)(2,1)} %orb_hbm.1, s32[1,512]{1,0:T(1,128)} %bitcast.2), custom_call_target="tpu_custom_call" | custom-call | tf_op jit(solution)/shard_map/pallas_call | solution.py:336
  27.8 1.0 %shard_map.29 = f32[16,128,128]{2,1,0:T(8,128)} custom-call(f32[8,128,128]{2,1,0:T(8,128)S(1)} %get-tuple-element.8.done, bf16[8,128,256]{2,1,0:T(8,128)(2,1)S(1)} %get-tuple-element.9.last, bf16[256,256]{1,0:T(8,128)(2,1)S(1)} %get-tuple-element.10.wide), custom_call_target="tpu_custom_call" | custom-call | tf_op jit(solution)/shard_map/pallas_call | solution.py:374

commit v7 on v6

--- a/solution.py
+++ b/solution.py
@@ -137,8 +137,6 @@
             for f in flavours:
                 line = (first_at[f] + e) % side
                 remote(theirs.at[f, line], from_sib.at[n, f], sib_send, sib_recv.at[n], sibling).start()
-        to_sibling = remote(phi.at[core], phi.at[core], orb_send, orb_recv, sibling)
-        to_sibling.start()
     with jax.named_scope("minepicks"):
         owned(mask_of(core), mine)
 
@@ -153,6 +151,9 @@
                     remote(
                         part.at[n, f], first_in.at[f, n], p_send.at[0], first_recv.at[f], along_first(f, e)
                     ).start()
+
+    to_sibling = remote(phi.at[core], phi.at[core], orb_send, orb_recv, sibling)
+    to_sibling.start()
 
     with jax.named_scope("tables"):
         high, low = split(cas_table())

time: 29 us -> 29 us (level)
  no operation moved by 1% of the time
where the time goes in v7:
time: 29 us; the launch traced here: 28.8 us
  Pallas kernels  28.8 us (99%)
    pallas_call x1, Pallas kernels, shards(): pl.pallas_call(functools.partial(body, side, points), out_shape=[jax.Shap...  27.8 us
    pallas_call x1, Pallas kernels, shards(): pl.pallas_call(finish, out_shape=jax.ShapeDtypeStruct((points, SIDE, SIDE...  1.03 us

profile of v7, /device:TPU:1, one launch (start us, length us, event | category | flops | bytes accessed | tf_op | source)
XLA Modules:
  0.0 28.8 jit_solution(3257151878475296571)
XLA Ops:
  0.0 27.8 %shard_map.28 = (f32[8,128,128]{2,1,0:T(8,128)S(1)}, bf16[8,128,256]{2,1,0:T(8,128)(2,1)S(1)}, bf16[256,256]{1,0:T(8,128)(2,1)S(1)}) custom-call(bf16[512,512]{1,0:T(8,128)(2,1)} %orb_hbm.1, s32[1,512]{1,0:T(1,128)} %bitcast.2), custom_call_target="tpu_custom_call" | custom-call | tf_op jit(solution)/shard_map/pallas_call | solution.py:337
  27.8 1.0 %shard_map.29 = f32[16,128,128]{2,1,0:T(8,128)} custom-call(f32[8,128,128]{2,1,0:T(8,128)S(1)} %get-tuple-element.8.done, bf16[8,128,256]{2,1,0:T(8,128)(2,1)S(1)} %get-tuple-element.9.last, bf16[256,256]{1,0:T(8,128)(2,1)S(1)} %get-tuple-element.10.wide), custom_call_target="tpu_custom_call" | custom-call | tf_op jit(solution)/shard_map/pallas_call | solution.py:375

commit v8 on v7

--- a/solution.py
+++ b/solution.py
@@ -167,32 +167,38 @@
         tall[SIDE:, SIDE:] = low
         kern[...] = screen_kernel()
 
+    def homes(h):
+        return pl.ds(h * (side // 2), side // 2)
+
+    halves = range(2)
     own_line = len(steps)
     for f in flavours:
         with jax.named_scope("firstwait%d" % f):
             wait_all(first_in.at[f], first_recv.at[f])
         with jax.named_scope("second%d" % f):
-            value = part[own_line, f]
-            for n in range(len(steps)):
-                value = value + first_in[f, n]
-            summed[f] = value
-            for n, e in enumerate(steps):
-                remote(
-                    summed.at[f], second_in.at[f, n], p_send.at[1], second_recv.at[f], along_second(f, e)
-                ).start()
-    for f in flavours:
-        with jax.named_scope("secondwait%d" % f):
-            wait_all(second_in.at[f], second_recv.at[f])
-        with jax.named_scope("third%d" % f):
-            value = summed[f]
-            for n in range(len(steps)):
-                value = value + second_in[f, n]
-            line = first_at[f]
-            vectors[f, line] = value
-            for e in steps:
-                remote(
-                    vectors.at[f, line], vectors.at[f, line], p_send.at[2], third_recv.at[f], along_first(f, e)
-                ).start()
+            for h in halves:
+                value = part[own_line, f, homes(h)]
+                for n in range(len(steps)):
+                    value = value + first_in[f, n, homes(h)]
+                summed[f, h] = value
+                for n, e in enumerate(steps):
+                    remote(
+                        summed.at[f, h], second_in.at[f, h, n], p_send.at[1], second_recv.at[f, h],
+                        along_second(f, e),
+                    ).start()
+    for h in halves:
+        for f in flavours:
+            with jax.named_scope("secondwait%d%d" % (h, f)):
+                wait_all(second_in.at[f, h], second_recv.at[f, h])
+            with jax.named_scope("third%d%d" % (h, f)):
+                value = summed[f, h]
+                for n in range(len(steps)):
+                    value = value + second_in[f, h, n]
+                line = first_at[f]
+                vectors[f, line, homes(h)] = value
+                for e in steps:
+                    here = vectors.at[f, line, homes(h)]
+                    remote(here, here, p_send.at[2], third_recv.at[f], along_first(f, e)).start()
 
     slots = [
         [o for o in offs if o[1 - f] == 0] + [o for o in offs if o[1 - f] != 0] for f in flavours
@@ -352,8 +358,8 @@
             pltpu.VMEM((side, 2, side, part_points, orbital_count), BF16),
             pltpu.VMEM((side, 2, side, part_points, orbital_count), BF16),
             pltpu.VMEM((2, side - 1, side, part_points, orbital_count), BF16),
-            pltpu.VMEM((2, side, part_points, orbital_count), BF16),
-            pltpu.VMEM((2, side - 1, side, part_points, orbital_count), BF16),
+            pltpu.VMEM((2, 2, side // 2, part_points, orbital_count), BF16),
+            pltpu.VMEM((2, 2, side - 1, side // 2, part_points, orbital_count), BF16),
             pltpu.VMEM((2, side, side, part_points, orbital_count), BF16),
             pltpu.VMEM((2, side, side, part_points, 2 * cells), jnp.int16),
             pltpu.VMEM((2, side, side, 1, SIDE), F32),
@@ -365,7 +371,7 @@
             pltpu.VMEM((2, part_points // 2, 2 * SIDE, 2 * SIDE), BF16),
             pltpu.VMEM((part_points, SIDE, 2 * SIDE), BF16),
             dma((2,)), dma, dma((side,)), dma, dma,
-            dma((3,)), dma((2,)), dma((2,)), dma((2,)),
+            dma((3,)), dma((2,)), dma((2, 2)), dma((2,)),
             dma, dma((2, groups)), dma, dma((2, groups)),
         ],
         compiler_params=pltpu.CompilerParams(

time: 29 us -> 28.8 us (level)
  the two profiles are of different devices: /device:TPU:1 before, /device:TPU:2 now
where the time goes in v8:
time: 28.8 us; the launch traced here: 28.7 us
  Pallas kernels  28.6 us (99%)
    pallas_call x1, Pallas kernels, shards(): pl.pallas_call(functools.partial(body, side, points), out_shape=[jax.Shap...  27.6 us
    pallas_call x1, Pallas kernels, shards(): pl.pallas_call(finish, out_shape=jax.ShapeDtypeStruct((points, SIDE, SIDE...  1.03 us

profile of v8, /device:TPU:2, one launch (start us, length us, event | category | flops | bytes accessed | tf_op | source)
XLA Modules:
  0.0 28.7 jit_solution(462566429243295945)
XLA Ops:
  0.0 27.6 %shard_map.28 = (f32[8,128,128]{2,1,0:T(8,128)S(1)}, bf16[8,128,256]{2,1,0:T(8,128)(2,1)S(1)}, bf16[256,256]{1,0:T(8,128)(2,1)S(1)}) custom-call(bf16[512,512]{1,0:T(8,128)(2,1)} %orb_hbm.1, s32[1,512]{1,0:T(1,128)} %bitcast.2), custom_call_target="tpu_custom_call" | custom-call | tf_op jit(solution)/shard_map/pallas_call | solution.py:343
  27.6 1.0 %shard_map.29 = f32[16,128,128]{2,1,0:T(8,128)} custom-call(f32[8,128,128]{2,1,0:T(8,128)S(1)} %get-tuple-element.8.done, bf16[8,128,256]{2,1,0:T(8,128)(2,1)S(1)} %get-tuple-element.9.last, bf16[256,256]{1,0:T(8,128)(2,1)S(1)} %get-tuple-element.10.wide), custom_call_target="tpu_custom_call" | custom-call | tf_op jit(solution)/shard_map/pallas_call | solution.py:381
